TPU v7x, 32 devices: a whole 2x2x4 slice. The times are simulated.
32 devices in a mesh: groups: 1, dev: 8 (over z, y), side: 4 (over x, core).
Axes of the slice: x: 2, y: 2, z: 4, core: 2. Of those that a mesh axis runs over, the one named last changes fastest.
Arguments:
- queries: bfloat16 [256, 4096], P(('groups', 'dev', 'side')), may hold values from -160 to 160
- kv_cache: bfloat16 [256, 192, 1024], P(('groups', 'dev', 'side')), may hold values from -4 to 4
- new_kv: bfloat16 [256, 1024], P(('groups', 'dev', 'side')), may hold values from -4 to 4
- lengths: int32 [256], P(('groups', 'dev', 'side')), may hold values from 24 to 192, as said below
- residual: bfloat16 [256, 2048], P(('groups', 'dev', 'side')), may hold values from -36 to 36
- w_out: bfloat16 [4096, 2048], P('side'), may hold values from -0.59765625 to 0.59765625
- norm_gain: float32 [2048], replicated, may hold values from 0.5 to 1.5
- expert_ids: int32 [256, 8], P(('groups', 'dev', 'side')), may hold values from 0 to 15, all different within a row; in each aligned block of 8 rows (0 to 7, 8 to 15, ...) at most 8 rows name the same one
- route_level: int32 [256, 8], P(('groups', 'dev', 'side')), may hold values from 1 to 255
- w_in: bfloat16 [32, 2048, 768], P(('dev', 'side')), may hold values from -0.125 to 0.125
- w_down: bfloat16 [32, 384, 2048], P(('dev', 'side')), may hold values from -0.4375 to 0.4375
Outputs:
- stream: bfloat16 [256, 2048], P(('groups', 'dev', 'side'))
- expert_sum: bfloat16 [256, 2048], P(('groups', 'dev', 'side'))
Inputs may be any that keep to these rules, and one draw needn't show every extreme that they name: `lengths`: in each aligned block of 8 requests some request has 192 cached tokens. `expert_ids`: A row names 8 different experts. In each aligned block of 8 rows no expert is named by more than 8 rows, and in some block some expert is named by exactly 8 rows.
All inputs are finite; a program needn't handle non-finite values.
Results may differ from a plain program's by a relative error of at most 0.013.
Values may be sent and summed in bfloat16 or wider, within the bound.
No kernel may reach another device: no remote copies, remote signals or barrier semaphores. Data moves between devices by JAX's collectives and lax.ppermute only.
A program may use at most 64 MiB of HBM per device.

v0:
```python
import math
import jax
import jax.numpy as jnp
from jax import lax
from jax.sharding import PartitionSpec as P

HQ = 32
KVH = 4
HD = 128
CACHE = 192


def partner(block, axis, bit):
    count = lax.axis_size(axis)
    route = []
    for low in range(count):
        high = low | 1 << bit
        if high != low and high < count:
            route += [(low, high), (high, low)]
    return lax.ppermute(block, axis, route)


def attend(queries, kv_cache, new_kv, lengths):
    req_rows = queries.shape[0]
    group_size = HQ // KVH
    split_at = KVH * HD
    grouped_q = queries.reshape(req_rows, KVH, group_size, HD)
    key_rows = kv_cache[:, :, :split_at].reshape(req_rows, CACHE, KVH, HD)
    value_rows = kv_cache[:, :, split_at:].reshape(req_rows, CACHE, KVH, HD)
    new_key = new_kv[:, :split_at].reshape(req_rows, KVH, HD)
    new_value = new_kv[:, split_at:].reshape(req_rows, KVH, HD)
    scaling = 1.0 / math.sqrt(HD)
    scores = (
        jnp.einsum("rgqd,rlgd->rgql", grouped_q, key_rows, preferred_element_type=jnp.float32)
        * scaling
    )
    own_score = (
        jnp.einsum("rgqd,rgd->rgq", grouped_q, new_key, preferred_element_type=jnp.float32)
        * scaling
    )
    visible = (jnp.arange(CACHE)[None, :] < lengths[:, None])[:, None, None, :]
    scores = jnp.where(visible, scores, -jnp.inf)
    peak = jnp.maximum(jnp.max(scores, axis=3), own_score)
    weights = jnp.where(visible, jnp.exp(scores - peak[..., None]), 0.0)
    own_weight = jnp.exp(own_score - peak)
    denominator = jnp.sum(weights, axis=3) + own_weight
    probability = (weights / denominator[..., None]).astype(jnp.bfloat16)
    own_prob = (own_weight / denominator).astype(jnp.bfloat16)
    mixed = jnp.einsum(
        "rgql,rlgd->rgqd", probability, value_rows, preferred_element_type=jnp.float32
    )
    mixed = (
        mixed
        + own_prob.astype(jnp.float32)[..., None] * new_value.astype(jnp.float32)[:, :, None, :]
    )
    return mixed.reshape(req_rows, HQ * HD).astype(jnp.bfloat16)


def expert_rows(received, gate_up_w, down_w):
    model_width = received.shape[2]
    flattened = received.reshape(-1, model_width)
    half_units = down_w.shape[0]
    gate_up = jnp.dot(flattened, gate_up_w, preferred_element_type=jnp.float32)
    hidden = (jax.nn.silu(gate_up[:, :half_units]) * gate_up[:, half_units:]).astype(jnp.bfloat16)
    result = jnp.dot(hidden, down_w, preferred_element_type=jnp.float32)
    return result.reshape(received.shape[0], received.shape[1], model_width)


def body(
    queries,
    kv_cache,
    new_kv,
    lengths,
    residual,
    w_out,
    norm_gain,
    expert_ids,
    route_level,
    w_in,
    w_down,
):
    req_rows = queries.shape[0]
    top_count = expert_ids.shape[1]
    model_width = residual.shape[1]
    attended = attend(queries, kv_cache, new_kv, lengths)
    columns = lax.all_to_all(attended, "side", split_axis=1, concat_axis=0, tiled=True)
    attention = lax.psum_scatter(
        jnp.dot(columns, w_out, preferred_element_type=jnp.float32),
        "side",
        scatter_dimension=0,
        tiled=True,
    )
    stream = residual.astype(jnp.float32) + attention
    mean_square = jnp.mean(stream * stream, axis=1, keepdims=True)
    normed = (stream * lax.rsqrt(mean_square + 1e-06) * norm_gain[None, :]).astype(jnp.bfloat16)
    shares = route_level.astype(jnp.float32)
    shares = shares / jnp.sum(shares, axis=1, keepdims=True)
    shards = lax.axis_size("dev") * lax.axis_size("side")
    experts = shards // 2
    capacity = 2 * req_rows * top_count // experts
    pair_expert = expert_ids.reshape(-1)
    one_hot = (pair_expert[:, None] == jnp.arange(experts, dtype=jnp.int32)[None, :]).astype(
        jnp.int32
    )
    slot_rank = jnp.sum((jnp.cumsum(one_hot, axis=0) - 1) * one_hot, axis=1)
    target = pair_expert * capacity + slot_rank
    placed = target[None, :] == jnp.arange(experts * capacity, dtype=jnp.int32)[:, None]
    placed = placed.reshape(experts * capacity, req_rows, top_count)
    picker = jnp.any(placed, axis=2).astype(jnp.bfloat16)
    mixing = jnp.sum(jnp.where(placed, shares[None, :, :], 0.0), axis=2).T
    outbox = jnp.dot(picker, normed, preferred_element_type=jnp.float32).astype(jnp.bfloat16)
    grouped = outbox.reshape(experts, capacity, model_width)
    pair_side = lax.axis_index("side") % 2
    gate_up_w = w_in[0]
    down_w = w_down[0]
    doubled = jnp.broadcast_to(grouped[:, None], (experts, 2, capacity, model_width))
    doubled = doubled.reshape(shards, capacity, model_width)
    partials = expert_rows(
        lax.all_to_all(doubled, ("dev", "side"), split_axis=0, concat_axis=0, tiled=True),
        gate_up_w,
        down_w,
    )
    halved = partials.reshape(shards, 2, capacity // 2, model_width)
    retained = jnp.where(pair_side == 0, halved[:, 0], halved[:, 1])
    handed = jnp.where(pair_side == 0, halved[:, 1], halved[:, 0])
    gained = partner(handed, "side", 0)
    joined = (retained + gained).astype(jnp.bfloat16)
    returned = lax.all_to_all(joined, ("dev", "side"), split_axis=0, concat_axis=0, tiled=True)
    outputs = returned.reshape(experts, capacity, model_width)
    expert_sum = jnp.dot(
        mixing,
        outputs.reshape(experts * capacity, model_width).astype(jnp.float32),
        precision=lax.Precision.HIGHEST,
    )
    return (stream.astype(jnp.bfloat16), expert_sum.astype(jnp.bfloat16))


def solution(mesh):
    return jax.shard_map(
        body,
        mesh=mesh,
        in_specs=(
            P(("groups", "dev", "side"), None),
            P(("groups", "dev", "side"), None, None),
            P(("groups", "dev", "side"), None),
            P(("groups", "dev", "side")),
            P(("groups", "dev", "side"), None),
            P("side", None),
            P(),
            P(("groups", "dev", "side"), None),
            P(("groups", "dev", "side"), None),
            P(("dev", "side"), None, None),
            P(("dev", "side"), None, None),
        ),
        out_specs=(P(("groups", "dev", "side"), None), P(("groups", "dev", "side"), None)),
        check_vma=False,
    )
```

profile of v0, /device:TPU:0, one launch (start us, length us, event | category | flops | bytes accessed | tf_op | source)
XLA Modules:
  0.0 121.0 jit_solution(14539800376660734263)
XLA Ops:
  7.2 0.9 iota_compare_fusion.2
  8.1 0.8 bitcast_convert_fusion
  8.9 2.5 %slice_bitcast_fusion.1 = (bf16[8,24,4,8,128]{4,3,2,1,0:T(8,128)(2,1)S(1)}, bf16[8,24,4,8,128]{4,3,2,1,0:T(8,128)(2,1)S(1)}) fusion(bf16[8,192,1024]{2,1,0:T(8,128)(2,1)} %param.12), kind=kLoop, calls=%fused_computation.14 | loop fusion | bytes 6291456
  11.5 1.0 fusion.46
  12.5 0.2 fusion.26
  12.8 0.6 fusion.20
  13.4 0.6 copy.34
  14.0 4.2 %all-to-all-start = ((bf16[8,4,1024]{2,0,1:T(8,128)(2,1)}), bf16[8,4,1024]{2,0,1:T(8,128)(2,1)S(1)}, u32[]{:S(2)}, u32[]{:S(2)}) async-start(bf16[8,4,1024]{2,0,1:T(8,128)(2,1)} %copy.34), calls=%async_computation | async-start | bytes 131072 | tf_op jit(solution)/shard_map/all_to_all | solution.py:86
  18.4 4.0 %all-to-all-done = bf16[8,4,1024]{2,0,1:T(8,128)(2,1)S(1)} async-done(((bf16[8,4,1024]{2,0,1:T(8,128)(2,1)}), bf16[8,4,1024]{2,0,1:T(8,128)(2,1)S(1)}, u32[]{:S(2)}, u32[]{:S(2)}) %all-to-all-start) | async-done | bytes 65568 | tf_op jit(solution)/shard_map/all_to_all | solution.py:86
  22.4 3.7 %fusion.32 = f32[32,2048]{1,0:T(8,128)} fusion(bf16[1024,2048]{1,0:T(8,128)(2,1)} %param.16, bf16[8,4,1024]{2,0,1:T(8,128)(2,1)S(1)} %all-to-all-done), kind=kOutput, calls=%fused_computation.33 | convolution fusion | flops 134217728 | bytes 4521984 | tf_op jit(solution)/shard_map/dot_general | solution.py:88
  26.7 20.5 %reduce-scatter.2.cloned.1.call-done = f32[8,2048]{1,0:T(8,128)} async-done(((f32[32,2048]{1,0:T(8,128)}), f32[8,2048]{1,0:T(8,128)}) %reduce-scatter.2.cloned.1.call-update) | async-done | bytes 65552 | tf_op jit(solution)/shard_map/reduce_scatter | solution.py:87
  47.2 1.6 %multiply_reduce_fusion = (f32[8]{0:T(128)S(1)}, bf16[8,2048]{1,0:T(8,128)(2,1)}) fusion(f32[8,2048]{1,0:T(8,128)} %reduce-scatter.2.cloned.1.call-done, bf16[8,2048]{1,0:T(8,128)(2,1)S(1)} %copy-done.1), kind=kLoop, calls=%fused_computation.36 | loop fusion | flops 81912 | bytes 131104 | tf_op jit(solution)/shard_map/reduce_sum | solution.py:94
  48.8 1.2 fusion.2
  50.0 1.2 broadcast_in_dim.57
  51.2 4.7 %all-to-all-start.1 = ((bf16[32,8,2048]{2,1,0:T(8,128)(2,1)}), bf16[32,8,2048]{2,1,0:T(8,128)(2,1)}, u32[]{:S(2)}, u32[]{:S(2)}) async-start(bf16[32,8,2048]{2,1,0:T(8,128)(2,1)} %bitcast.63), calls=%async_computation.2 | async-start | bytes 2097152 | tf_op jit(solution)/shard_map/all_to_all | solution.py:119
  55.9 26.2 %all-to-all-done.1 = bf16[32,8,2048]{2,1,0:T(8,128)(2,1)} async-done(((bf16[32,8,2048]{2,1,0:T(8,128)(2,1)}), bf16[32,8,2048]{2,1,0:T(8,128)(2,1)}, u32[]{:S(2)}, u32[]{:S(2)}) %all-to-all-start.1) | async-done | bytes 1048608 | tf_op jit(solution)/shard_map/all_to_all | solution.py:119
  82.1 2.2 %fusion = f32[256,768]{1,0:T(8,128)S(1)} fusion(bf16[1,2048,768]{2,1,0:T(8,128)(2,1)S(1)} %copy-done, bf16[32,8,2048]{2,1,0:T(8,128)(2,1)} %all-to-all-done.1), kind=kOutput, calls=%fused_computation | convolution fusion | flops 805306368 | bytes 4980736 | tf_op jit(solution)/shard_map/dot_general | solution.py:63
  84.5 2.1 %fusion.9 = f32[32,2,4,2048]{3,0,2,1:T(8,128)S(1)} fusion(bf16[1,384,2048]{2,1,0:T(8,128)(2,1)} %param.21, bf16[32,2,4,384]{3,2,1,0:T(4,128)(2,1)S(1)} %dot_general.32), kind=kOutput, calls=%fused_computation.11 | convolution fusion | flops 402653184 | bytes 3866624 | tf_op jit(solution)/shard_map/dot_general | solution.py:65
  86.8 2.6 %collective-permute-done = f32[32,4,2048]{2,0,1:T(8,128)S(1)} collective-permute-done((f32[32,4,2048]{2,0,1:T(8,128)S(1)}, f32[32,4,2048]{2,0,1:T(8,128)S(1)}, u32[]{:S(2)}, u32[]{:S(2)}) %collective-permute-start) | collective-permute-done | bytes 1048608 | tf_op jit(solution)/shard_map/ppermute | solution.py:20
  89.7 1.2 %copy.36 = bf16[32,4,2048]{2,1,0:T(4,128)(2,1)} copy(bf16[32,4,2048]{2,0,1:T(8,128)(2,1)S(1)} %fusion.23) | data formatting | bytes 1048576 | tf_op jit(solution)/shard_map/convert_element_type | solution.py:127
  90.9 3.7 %all-to-all-start.2 = ((bf16[32,4,2048]{2,1,0:T(4,128)(2,1)}), bf16[32,4,2048]{2,1,0:T(4,128)(2,1)}, u32[]{:S(2)}, u32[]{:S(2)}) async-start(bf16[32,4,2048]{2,1,0:T(4,128)(2,1)} %copy.36), calls=%async_computation.3 | async-start | bytes 1048576 | tf_op jit(solution)/shard_map/all_to_all | solution.py:128
  94.9 15.3 %all-to-all-done.2 = bf16[32,4,2048]{2,1,0:T(4,128)(2,1)} async-done(((bf16[32,4,2048]{2,1,0:T(4,128)(2,1)}), bf16[32,4,2048]{2,1,0:T(4,128)(2,1)}, u32[]{:S(2)}, u32[]{:S(2)}) %all-to-all-start.2) | async-done | bytes 524320 | tf_op jit(solution)/shard_map/all_to_all | solution.py:128
  110.2 2.0 %reshape_reshape.4 = bf16[128,2048]{1,0:T(8,128)(2,1)} reshape(bf16[32,4,2048]{2,1,0:T(4,128)(2,1)} %all-to-all-done.2) | data formatting | bytes 1048576 | tf_op jit(solution)/shard_map/reshape;reshape | solution.py:132
  112.2 2.0 %convolution_convert_fusion.1 = bf16[8,2048]{1,0:T(8,128)(2,1)} fusion(f32[128,8]{0,1:T(8,128)S(1)} %select_reduce_fusion, bf16[128,2048]{1,0:T(8,128)(2,1)} %reshape_reshape.4), kind=kOutput, calls=%fused_computation.4 | convolution fusion | flops 25182208 | bytes 561152 | tf_op jit(solution)/shard_map/dot_general | solution.py:130
  (35 shorter events, 1.7 us)
Async XLA Ops:
  7.2 74.9 %copy-start = (bf16[1,2048,768]{2,1,0:T(8,128)(2,1)S(1)}, bf16[1,2048,768]{2,1,0:T(8,128)(2,1)}, u32[]{:S(2)}) copy-start(bf16[1,2048,768]{2,1,0:T(8,128)(2,1)} %param.20) | copy-start | bytes 9437188
  8.9 2.5 %copy-start.2 = (bf16[8,4096]{1,0:T(8,128)(2,1)S(1)}, bf16[8,4096]{1,0:T(8,128)(2,1)}, u32[]{:S(2)}) copy-start(bf16[8,4096]{1,0:T(8,128)(2,1)} %param.11) | copy-start | bytes 196612
  12.8 5.5 %copy-start.3 = (s32[8,8]{1,0:T(8,128)S(1)}, s32[8,8]{1,0:T(8,128)}, u32[]{:S(2)}) copy-start(s32[8,8]{1,0:T(8,128)} %param.18) | copy-start | bytes 772
  14.0 8.4 %all-to-all-start = ((bf16[8,4,1024]{2,0,1:T(8,128)(2,1)}), bf16[8,4,1024]{2,0,1:T(8,128)(2,1)S(1)}, u32[]{:S(2)}, u32[]{:S(2)}) async-start(bf16[8,4,1024]{2,0,1:T(8,128)(2,1)} %copy.34), calls=%async_computation | async-start | bytes 131072 | tf_op jit(solution)/shard_map/all_to_all | solution.py:86
  18.3 28.9 %reduce-scatter.2.cloned.1.call-start = ((), (), s32[]{:S(2)}) async-start(), calls=%async_computation.4 | async-start | bytes 327680 | tf_op jit(solution)/shard_map/reduce_scatter | solution.py:87
  18.4 28.8 %copy-start.1 = (bf16[8,2048]{1,0:T(8,128)(2,1)S(1)}, bf16[8,2048]{1,0:T(8,128)(2,1)}, u32[]{:S(2)}) copy-start(bf16[8,2048]{1,0:T(8,128)(2,1)} %param.15) | copy-start | bytes 98308
  18.4 30.4 %copy-start.5 = (f32[2048]{0:T(1024)S(1)}, f32[2048]{0:T(1024)}, u32[]{:S(2)}) copy-start(f32[2048]{0:T(1024)} %param.17) | copy-start | bytes 24580
  51.2 30.9 %all-to-all-start.1 = ((bf16[32,8,2048]{2,1,0:T(8,128)(2,1)}), bf16[32,8,2048]{2,1,0:T(8,128)(2,1)}, u32[]{:S(2)}, u32[]{:S(2)}) async-start(bf16[32,8,2048]{2,1,0:T(8,128)(2,1)} %bitcast.63), calls=%async_computation.2 | async-start | bytes 2097152 | tf_op jit(solution)/shard_map/all_to_all | solution.py:119
  86.7 2.7 %collective-permute-start = (f32[32,4,2048]{2,0,1:T(8,128)S(1)}, f32[32,4,2048]{2,0,1:T(8,128)S(1)}, u32[]{:S(2)}, u32[]{:S(2)}) collective-permute-start(f32[32,4,2048]{2,0,1:T(8,128)S(1)} %select_bitcast_fusion), channel_id=1, source_target_pairs={{0,1},{1,0},{2,3},{3,2},{4,5},{5,4},{6,7},{7,6},{8,9},{9,8},{10,11... | collective-permute-start | bytes 3145736 | tf_op jit(solution)/shard_map/ppermute | solution.py:20
  89.6 5.0 %copy-start.4 = (s32[8,8]{1,0:T(8,128)S(1)}, s32[8,8]{1,0:T(8,128)}, u32[]{:S(2)}) copy-start(s32[8,8]{1,0:T(8,128)} %param.19) | copy-start | bytes 772
  90.9 19.3 %all-to-all-start.2 = ((bf16[32,4,2048]{2,1,0:T(4,128)(2,1)}), bf16[32,4,2048]{2,1,0:T(4,128)(2,1)}, u32[]{:S(2)}, u32[]{:S(2)}) async-start(bf16[32,4,2048]{2,1,0:T(4,128)(2,1)} %copy.36), calls=%async_computation.3 | async-start | bytes 1048576 | tf_op jit(solution)/shard_map/all_to_all | solution.py:128
Sparse Core Ops, SparseCore 0:
  26.3 20.8 reduce-scatter.1
where the time goes:
time: 122 us; the launch traced here: 121 us
  waiting for transfers between devices  68.7 us (56%)
  between operations  14.2 us (12%)
  matrix products  12.9 us (11%)
  starting transfers between devices  12.8 us (10%)
  local copies, waits for them, and re-layouts  7.73 us (6%)
  other arithmetic  4.69 us (4%)
    all_to_all x1, waiting for transfers between devices, body(): lax.all_to_all(doubled, ('dev', 'side'), split_axis=0, concat_axis=0, til...  26.2 us
    reduce_scatter x1, waiting for transfers between devices, body(): lax.psum_scatter(jnp.dot(columns, w_out, preferred_element_type=jnp.float...  20.5 us
    all_to_all x1, waiting for transfers between devices, body(): lax.all_to_all(joined, ('dev', 'side'), split_axis=0, concat_axis=0, tile...  15.3 us
    all_to_all x1, starting transfers between devices, body(): lax.all_to_all(doubled, ('dev', 'side'), split_axis=0, concat_axis=0, til...  4.73 us
    all_to_all x1, starting transfers between devices, body(): lax.all_to_all(attended, 'side', split_axis=1, concat_axis=0, tiled=True)  4.24 us
    all_to_all x1, waiting for transfers between devices, body(): lax.all_to_all(attended, 'side', split_axis=1, concat_axis=0, tiled=True)  4.03 us
    all_to_all x1, starting transfers between devices, body(): lax.all_to_all(joined, ('dev', 'side'), split_axis=0, concat_axis=0, tile...  3.75 us
    dot_general x1, matrix products, body(): jnp.dot(columns, w_out, preferred_element_type=jnp.float32)  3.71 us
  transfers between devices with their start and end apart: 5, of which 5 were waited for; matrix products, arithmetic and copies ran while one was open for 1% of the time, Pallas kernels for 0%

commit v1 on v0

--- a/solution.py
+++ b/solution.py
@@ -83,7 +83,10 @@
     top_count = expert_ids.shape[1]
     model_width = residual.shape[1]
     attended = attend(queries, kv_cache, new_kv, lengths)
-    columns = lax.all_to_all(attended, "side", split_axis=1, concat_axis=0, tiled=True)
+    columns = jnp.concatenate(
+        lax.all_to_all(jnp.stack(jnp.split(attended, lax.axis_size("side"), axis=1)), "side", 0, 0),
+        axis=0,
+    )
     attention = lax.psum_scatter(
         jnp.dot(columns, w_out, preferred_element_type=jnp.float32),
         "side",

time: 122 us -> 122 us (level)
    unnamed x13 -> x14, local copies, waits for them, and re-layouts: 2.49 us -> 2.52 us
where the time goes in v1:
time: 122 us; the launch traced here: 121 us
  waiting for transfers between devices  68.7 us (56%)
  between operations  14.2 us (12%)
  matrix products  12.9 us (11%)
  starting transfers between devices  12.8 us (10%)
  local copies, waits for them, and re-layouts  7.1 us (6%)
  other arithmetic  5.32 us (4%)
    all_to_all x1, waiting for transfers between devices, body(): lax.all_to_all(doubled, ('dev', 'side'), split_axis=0, concat_axis=0, til...  26.2 us
    reduce_scatter x1, waiting for transfers between devices, body(): lax.psum_scatter(jnp.dot(columns, w_out, preferred_element_type=jnp.float...  20.5 us
    all_to_all x1, waiting for transfers between devices, body(): lax.all_to_all(joined, ('dev', 'side'), split_axis=0, concat_axis=0, tile...  15.3 us
    all_to_all x1, starting transfers between devices, body(): lax.all_to_all(doubled, ('dev', 'side'), split_axis=0, concat_axis=0, til...  4.73 us
    all_to_all x1, starting transfers between devices, body(): lax.all_to_all(jnp.stack(jnp.split(attended, lax.axis_size('side'), axis=...  4.24 us
    all_to_all x1, waiting for transfers between devices, body(): lax.all_to_all(jnp.stack(jnp.split(attended, lax.axis_size('side'), axis=...  4.03 us
    all_to_all x1, starting transfers between devices, body(): lax.all_to_all(joined, ('dev', 'side'), split_axis=0, concat_axis=0, tile...  3.75 us
    dot_general x1, matrix products, body(): jnp.dot(columns, w_out, preferred_element_type=jnp.float32)  3.71 us
  transfers between devices with their start and end apart: 5, of which 5 were waited for; matrix products, arithmetic and copies ran while one was open for 1% of the time, Pallas kernels for 0%

profile of v1, /device:TPU:0, one launch (start us, length us, event | category | flops | bytes accessed | tf_op | source)
XLA Modules:
  0.0 121.0 jit_solution(16230861676966407993)
XLA Ops:
  7.2 0.9 iota_compare_fusion.2
  8.1 0.8 bitcast_convert_fusion
  8.9 2.5 %slice_bitcast_fusion.1 = (bf16[8,24,4,8,128]{4,3,2,1,0:T(8,128)(2,1)S(1)}, bf16[8,24,4,8,128]{4,3,2,1,0:T(8,128)(2,1)S(1)}) fusion(bf16[8,192,1024]{2,1,0:T(8,128)(2,1)} %param.12), kind=kLoop, calls=%fused_computation.14 | loop fusion | bytes 6291456
  11.5 1.0 fusion.49
  12.5 0.2 fusion.29
  12.8 0.6 fusion.23
  13.4 0.6 pad_maximum_fusion
  14.1 4.2 %all-to-all-start = ((bf16[4,8,1024]{2,1,0:T(8,128)(2,1)}), bf16[4,8,1024]{2,1,0:T(8,128)(2,1)S(1)}, u32[]{:S(2)}, u32[]{:S(2)}) async-start(bf16[4,8,1024]{2,1,0:T(8,128)(2,1)} %pad_maximum_fusion), calls=%async_computation | async-start | bytes 131072 | tf_op jit(solution)/shard_map/all_to_all | solution.py:87
  18.4 4.0 %all-to-all-done = bf16[4,8,1024]{2,1,0:T(8,128)(2,1)S(1)} async-done(((bf16[4,8,1024]{2,1,0:T(8,128)(2,1)}), bf16[4,8,1024]{2,1,0:T(8,128)(2,1)S(1)}, u32[]{:S(2)}, u32[]{:S(2)}) %all-to-all-start) | async-done | bytes 65568 | tf_op jit(solution)/shard_map/all_to_all | solution.py:87
  22.4 3.7 %fusion.35 = f32[32,2048]{1,0:T(8,128)} fusion(bf16[1024,2048]{1,0:T(8,128)(2,1)} %param.16, bf16[4,8,1024]{2,1,0:T(8,128)(2,1)S(1)} %all-to-all-done), kind=kOutput, calls=%fused_computation.36 | convolution fusion | flops 134217728 | bytes 4521984 | tf_op jit(solution)/shard_map/dot_general | solution.py:91
  26.7 20.5 %reduce-scatter.2.cloned.1.call-done = f32[8,2048]{1,0:T(8,128)} async-done(((f32[32,2048]{1,0:T(8,128)}), f32[8,2048]{1,0:T(8,128)}) %reduce-scatter.2.cloned.1.call-update) | async-done | bytes 65552 | tf_op jit(solution)/shard_map/reduce_scatter | solution.py:90
  47.2 1.6 %multiply_reduce_fusion = (f32[8]{0:T(128)S(1)}, bf16[8,2048]{1,0:T(8,128)(2,1)}) fusion(f32[8,2048]{1,0:T(8,128)} %reduce-scatter.2.cloned.1.call-done, bf16[8,2048]{1,0:T(8,128)(2,1)S(1)} %copy-done.1), kind=kLoop, calls=%fused_computation.39 | loop fusion | flops 81912 | bytes 131104 | tf_op jit(solution)/shard_map/reduce_sum | solution.py:97
  48.8 1.2 fusion.2
  50.0 1.2 broadcast_in_dim.57
  51.2 4.7 %all-to-all-start.1 = ((bf16[32,8,2048]{2,1,0:T(8,128)(2,1)}), bf16[32,8,2048]{2,1,0:T(8,128)(2,1)}, u32[]{:S(2)}, u32[]{:S(2)}) async-start(bf16[32,8,2048]{2,1,0:T(8,128)(2,1)} %bitcast.75), calls=%async_computation.2 | async-start | bytes 2097152 | tf_op jit(solution)/shard_map/all_to_all | solution.py:122
  55.9 26.2 %all-to-all-done.1 = bf16[32,8,2048]{2,1,0:T(8,128)(2,1)} async-done(((bf16[32,8,2048]{2,1,0:T(8,128)(2,1)}), bf16[32,8,2048]{2,1,0:T(8,128)(2,1)}, u32[]{:S(2)}, u32[]{:S(2)}) %all-to-all-start.1) | async-done | bytes 1048608 | tf_op jit(solution)/shard_map/all_to_all | solution.py:122
  82.1 2.2 %fusion = f32[256,768]{1,0:T(8,128)S(1)} fusion(bf16[1,2048,768]{2,1,0:T(8,128)(2,1)S(1)} %copy-done, bf16[32,8,2048]{2,1,0:T(8,128)(2,1)} %all-to-all-done.1), kind=kOutput, calls=%fused_computation | convolution fusion | flops 805306368 | bytes 4980736 | tf_op jit(solution)/shard_map/dot_general | solution.py:63
  84.5 2.1 %fusion.9 = f32[32,2,4,2048]{3,0,2,1:T(8,128)S(1)} fusion(bf16[1,384,2048]{2,1,0:T(8,128)(2,1)} %param.21, bf16[32,2,4,384]{3,2,1,0:T(4,128)(2,1)S(1)} %dot_general.32), kind=kOutput, calls=%fused_computation.11 | convolution fusion | flops 402653184 | bytes 3866624 | tf_op jit(solution)/shard_map/dot_general | solution.py:65
  86.8 2.6 %collective-permute-done = f32[32,4,2048]{2,0,1:T(8,128)S(1)} collective-permute-done((f32[32,4,2048]{2,0,1:T(8,128)S(1)}, f32[32,4,2048]{2,0,1:T(8,128)S(1)}, u32[]{:S(2)}, u32[]{:S(2)}) %collective-permute-start) | collective-permute-done | bytes 1048608 | tf_op jit(solution)/shard_map/ppermute | solution.py:20
  89.7 1.2 %copy.33 = bf16[32,4,2048]{2,1,0:T(4,128)(2,1)} copy(bf16[32,4,2048]{2,0,1:T(8,128)(2,1)S(1)} %fusion.26) | data formatting | bytes 1048576 | tf_op jit(solution)/shard_map/convert_element_type | solution.py:130
  90.9 3.7 %all-to-all-start.2 = ((bf16[32,4,2048]{2,1,0:T(4,128)(2,1)}), bf16[32,4,2048]{2,1,0:T(4,128)(2,1)}, u32[]{:S(2)}, u32[]{:S(2)}) async-start(bf16[32,4,2048]{2,1,0:T(4,128)(2,1)} %copy.33), calls=%async_computation.3 | async-start | bytes 1048576 | tf_op jit(solution)/shard_map/all_to_all | solution.py:131
  94.9 15.3 %all-to-all-done.2 = bf16[32,4,2048]{2,1,0:T(4,128)(2,1)} async-done(((bf16[32,4,2048]{2,1,0:T(4,128)(2,1)}), bf16[32,4,2048]{2,1,0:T(4,128)(2,1)}, u32[]{:S(2)}, u32[]{:S(2)}) %all-to-all-start.2) | async-done | bytes 524320 | tf_op jit(solution)/shard_map/all_to_all | solution.py:131
  110.2 2.0 %reshape_reshape.4 = bf16[128,2048]{1,0:T(8,128)(2,1)} reshape(bf16[32,4,2048]{2,1,0:T(4,128)(2,1)} %all-to-all-done.2) | data formatting | bytes 1048576 | tf_op jit(solution)/shard_map/reshape;reshape | solution.py:135
  112.2 2.0 %convolution_convert_fusion.1 = bf16[8,2048]{1,0:T(8,128)(2,1)} fusion(f32[128,8]{0,1:T(8,128)S(1)} %select_reduce_fusion, bf16[128,2048]{1,0:T(8,128)(2,1)} %reshape_reshape.4), kind=kOutput, calls=%fused_computation.4 | convolution fusion | flops 25182208 | bytes 561152 | tf_op jit(solution)/shard_map/dot_general | solution.py:133
  (36 shorter events, 1.8 us)
Async XLA Ops:
  7.2 74.9 %copy-start = (bf16[1,2048,768]{2,1,0:T(8,128)(2,1)S(1)}, bf16[1,2048,768]{2,1,0:T(8,128)(2,1)}, u32[]{:S(2)}) copy-start(bf16[1,2048,768]{2,1,0:T(8,128)(2,1)} %param.20) | copy-start | bytes 9437188
  8.9 2.5 %copy-start.2 = (bf16[8,4096]{1,0:T(8,128)(2,1)S(1)}, bf16[8,4096]{1,0:T(8,128)(2,1)}, u32[]{:S(2)}) copy-start(bf16[8,4096]{1,0:T(8,128)(2,1)} %param.11) | copy-start | bytes 196612
  12.8 5.5 %copy-start.3 = (s32[8,8]{1,0:T(8,128)S(1)}, s32[8,8]{1,0:T(8,128)}, u32[]{:S(2)}) copy-start(s32[8,8]{1,0:T(8,128)} %param.18) | copy-start | bytes 772
  14.1 8.4 %all-to-all-start = ((bf16[4,8,1024]{2,1,0:T(8,128)(2,1)}), bf16[4,8,1024]{2,1,0:T(8,128)(2,1)S(1)}, u32[]{:S(2)}, u32[]{:S(2)}) async-start(bf16[4,8,1024]{2,1,0:T(8,128)(2,1)} %pad_maximum_fusion), calls=%async_computation | async-start | bytes 131072 | tf_op jit(solution)/shard_map/all_to_all | solution.py:87
  18.3 28.9 %reduce-scatter.2.cloned.1.call-start = ((), (), s32[]{:S(2)}) async-start(), calls=%async_computation.4 | async-start | bytes 327680 | tf_op jit(solution)/shard_map/reduce_scatter | solution.py:90
  18.4 28.8 %copy-start.1 = (bf16[8,2048]{1,0:T(8,128)(2,1)S(1)}, bf16[8,2048]{1,0:T(8,128)(2,1)}, u32[]{:S(2)}) copy-start(bf16[8,2048]{1,0:T(8,128)(2,1)} %param.15) | copy-start | bytes 98308
  18.4 30.4 %copy-start.5 = (f32[2048]{0:T(1024)S(1)}, f32[2048]{0:T(1024)}, u32[]{:S(2)}) copy-start(f32[2048]{0:T(1024)} %param.17) | copy-start | bytes 24580
  51.2 30.9 %all-to-all-start.1 = ((bf16[32,8,2048]{2,1,0:T(8,128)(2,1)}), bf16[32,8,2048]{2,1,0:T(8,128)(2,1)}, u32[]{:S(2)}, u32[]{:S(2)}) async-start(bf16[32,8,2048]{2,1,0:T(8,128)(2,1)} %bitcast.75), calls=%async_computation.2 | async-start | bytes 2097152 | tf_op jit(solution)/shard_map/all_to_all | solution.py:122
  86.7 2.7 %collective-permute-start = (f32[32,4,2048]{2,0,1:T(8,128)S(1)}, f32[32,4,2048]{2,0,1:T(8,128)S(1)}, u32[]{:S(2)}, u32[]{:S(2)}) collective-permute-start(f32[32,4,2048]{2,0,1:T(8,128)S(1)} %select_bitcast_fusion), channel_id=1, source_target_pairs={{0,1},{1,0},{2,3},{3,2},{4,5},{5,4},{6,7},{7,6},{8,9},{9,8},{10,11... | collective-permute-start | bytes 3145736 | tf_op jit(solution)/shard_map/ppermute | solution.py:20
  89.6 5.0 %copy-start.4 = (s32[8,8]{1,0:T(8,128)S(1)}, s32[8,8]{1,0:T(8,128)}, u32[]{:S(2)}) copy-start(s32[8,8]{1,0:T(8,128)} %param.19) | copy-start | bytes 772
  90.9 19.3 %all-to-all-start.2 = ((bf16[32,4,2048]{2,1,0:T(4,128)(2,1)}), bf16[32,4,2048]{2,1,0:T(4,128)(2,1)}, u32[]{:S(2)}, u32[]{:S(2)}) async-start(bf16[32,4,2048]{2,1,0:T(4,128)(2,1)} %copy.33), calls=%async_computation.3 | async-start | bytes 1048576 | tf_op jit(solution)/shard_map/all_to_all | solution.py:131
Sparse Core Ops, SparseCore 0:
  26.3 20.8 reduce-scatter.1
